TPU v7x, 128 devices: a whole 4x4x4 slice. The times are simulated.
128 devices in a mesh: wide: 8 (over x, core), rep: 16 (over y, z).
Axes of the slice: x: 4, y: 4, z: 4, core: 2. Of those that a mesh axis runs over, the one named last changes fastest.
Arguments:
- stretch_qkv: bfloat16 [16, 1536, 3, 5120], P('rep', 'wide'), may hold values from -60 to 60
- norm_gains: float32 [2, 5120], replicated, may hold values from 0.25 to 1.75
- cache: bfloat16 [256, 2, 192, 5120], P('rep', None, 'wide'), may hold values from -6 to 6
- cached_stretches: int32 [16], replicated, may hold values from 1 to 2, as said below
- block_slot: int32 [16, 16], replicated, may hold values from 0 to 255, as said below
- video_of_group: int32 [16], replicated, may hold values from 0 to 15, each once
Outputs:
- attended: bfloat16 [16, 1536, 5120], P('rep', 'wide')
Inputs may be any that keep to these rules, and one draw needn't show every extreme that they name: `cached_stretches`: each value is 1 to 2; some video has exactly 2. Block b of video u holds that video's cached tokens b * 192 to (b + 1) * 192 - 1, oldest first; it is cache row block_slot[u, b], owned by group block_slot[u, b] // 16. Every group owns exactly 1 block of every video; no two blocks share a row.
All inputs are finite; a program needn't handle non-finite values.
Results may differ from a plain program's by a relative error of at most 0.011.
Values may be sent and summed in bfloat16 or wider, within the bound.
A program may use at most 128 MiB of HBM per device.

v0:
```python
import math

import jax
import jax.numpy as jnp
from jax import lax
from jax.sharding import PartitionSpec as P

HD = 128


epsilon = 1e-06


def normalize(stretch_rows, gains_row):
    widened = stretch_rows.astype(jnp.float32)
    mean_square = jnp.mean(widened * widened, axis=-1, keepdims=True)
    return (widened * lax.rsqrt(mean_square + epsilon) * gains_row).astype(jnp.bfloat16)


def attend_block(query_rows, all_keys, all_values, usable):
    scores = jnp.einsum(
        "qhd,khd->hqk", query_rows, all_keys, preferred_element_type=jnp.float32
    ) * HD ** (-0.5)
    scores = jnp.where(usable[None, None, :], scores, -jnp.inf)
    row_max = jnp.max(scores, axis=-1, keepdims=True)
    weights = jnp.exp(scores - row_max)
    row_total = jnp.sum(weights, axis=-1, keepdims=True)
    mixed = jnp.einsum(
        "hqk,khd->qhd", weights.astype(jnp.bfloat16), all_values, preferred_element_type=jnp.float32
    )
    return (mixed / jnp.transpose(row_total, (1, 0, 2))).astype(jnp.bfloat16)


def body(stretch_qkv, norm_gains, cache, cached_stretches, block_slot, video_of_group):
    rep_count = lax.axis_size("rep")
    wide_count = lax.axis_size("wide")
    own_group = lax.axis_index("rep")
    stretch_rows = stretch_qkv[0]
    width = stretch_rows.shape[-1]
    head_width = width // wide_count
    heads_dev = head_width // HD
    queries = normalize(stretch_rows[:, 0], norm_gains[0])
    keys_new = normalize(stretch_rows[:, 1], norm_gains[1])
    framed = jnp.stack([queries, keys_new, stretch_rows[:, 2]], axis=1)
    headed = lax.all_to_all(framed, "wide", split_axis=2, concat_axis=0, tiled=True)
    stretch_len = headed.shape[0]
    slots_dev = cache.shape[0]
    cap_dev = slots_dev // rep_count
    blocks = block_slot.shape[1]
    block_wide = cache.shape[2]
    block_len = block_wide * wide_count
    group_ids = jnp.arange(rep_count, dtype=jnp.int32)
    pick_video = (video_of_group[:, None] == group_ids[None, :]).astype(jnp.int32)
    slot_table = jnp.dot(pick_video, block_slot)
    owned_here = (slot_table // slots_dev == own_group).astype(jnp.int32)
    rank_in_owner = jnp.cumsum(owned_here, axis=1) - owned_here
    local_slot = slot_table % slots_dev
    chosen = jnp.stack([jnp.sum(owned_here * (rank_in_owner == 0) * local_slot, axis=1)], axis=1)
    outgoing = cache[chosen.reshape(-1)].reshape((rep_count, cap_dev) + cache.shape[1:])
    split_heads = outgoing.reshape(rep_count, cap_dev, 2, block_wide, wide_count, head_width)
    moved = jnp.moveaxis(split_heads, 4, 0).reshape(
        wide_count * rep_count, cap_dev, 2, block_wide, head_width
    )
    received = lax.all_to_all(moved, ("wide", "rep"), split_axis=0, concat_axis=0, tiled=True)
    received = received.reshape(wide_count, rep_count, cap_dev, 2, block_wide, head_width)
    arrived = jnp.transpose(received, (1, 2, 3, 0, 4, 5)).reshape(
        rep_count, cap_dev, 2, block_len, head_width
    )
    is_me = (group_ids == own_group).astype(jnp.int32)
    own_table = jnp.sum(slot_table * is_me[:, None], axis=0)
    own_video = jnp.sum(video_of_group * is_me)
    own_count = jnp.sum(cached_stretches * (group_ids == own_video).astype(jnp.int32))
    owners = own_table // slots_dev
    block_order = jnp.arange(blocks, dtype=jnp.int32)
    before = jnp.sum(
        (
            (owners[:, None] == owners[None, :]) & (block_order[:, None] > block_order[None, :])
        ).astype(jnp.int32),
        axis=1,
    )
    flat_index = owners * cap_dev + before
    history = arrived.reshape((rep_count * cap_dev,) + arrived.shape[2:])[flat_index]
    hist_span = blocks * block_len
    hist_keys = history[:, 0].reshape(hist_span, heads_dev, HD)
    hist_values = history[:, 1].reshape(hist_span, heads_dev, HD)
    new_queries = headed[:, 0].reshape(stretch_len, heads_dev, HD)
    new_keys = headed[:, 1].reshape(stretch_len, heads_dev, HD)
    new_values = headed[:, 2].reshape(stretch_len, heads_dev, HD)
    query_block = math.gcd(stretch_len, 256)
    blocks_q = new_queries.reshape(stretch_len // query_block, query_block, heads_dev, HD)
    all_keys = jnp.concatenate([hist_keys, new_keys], axis=0)
    all_values = jnp.concatenate([hist_values, new_values], axis=0)
    key_position = jnp.arange(hist_span + stretch_len, dtype=jnp.int32)
    usable = (key_position < own_count * stretch_len) | (key_position >= hist_span)
    attended = lax.map(lambda piece: attend_block(piece, all_keys, all_values, usable), blocks_q)
    attended = attended.reshape(stretch_len, head_width)
    returned = lax.all_to_all(attended, "wide", split_axis=0, concat_axis=1, tiled=True)
    return returned[None]


def solution(mesh):
    in_specs = (P("rep", "wide", None, None), P(), P("rep", None, "wide", None), P(), P(), P())
    out_specs = P("rep", "wide", None)
    return jax.shard_map(body, mesh=mesh, in_specs=in_specs, out_specs=out_specs, check_vma=False)
```

profile of v0, /device:TPU:1, one launch (start us, length us, event | category | flops | bytes accessed | tf_op | source)
XLA Modules:
  0.0 599.0 jit_solution(7813864269104856117)
XLA Ops:
  0.0 3.1 fusion.30
  6.2 3.0 pad_maximum_fusion
  9.2 15.6 %copy.77 = bf16[192,3,5120]{0,1,2:T(4,128)(2,1)} copy(bf16[192,3,5120]{2,0,1:T(8,128)(2,1)} %pad_maximum_fusion) | data formatting | bytes 11796480 | tf_op jit(solution)/shard_map/stack | solution.py:44
  24.8 6.5 %all-to-all-start = ((bf16[192,3,5120]{0,1,2:T(4,128)(2,1)}), bf16[192,3,5120]{0,1,2:T(4,128)(2,1)}, u32[]{:S(2)}, u32[]{:S(2)}) async-start(bf16[192,3,5120]{0,1,2:T(4,128)(2,1)} %copy.77), calls=%async_computation | async-start | bytes 20971520 | tf_op jit(solution)/shard_map/all_to_all | solution.py:45
  31.9 7.9 %gather_fusion = bf16[16,2,24,5120]{3,2,1,0:T(8,128)(2,1)} fusion(bf16[16,2,24,5120]{3,2,1,0:T(8,128)(2,1)} %param.10, s32[1024]{0:T(1024)S(1)} %pad_clamp_fusion.1), kind=kCustom, calls=%fused_computation | custom fusion | bytes 15728704 | tf_op jit(solution)/shard_map/gather | solution.py:59
  39.8 5.1 copy.97
  44.9 4.2 copy.81
  49.0 98.5 %all-to-all-done = bf16[192,3,5120]{0,1,2:T(4,128)(2,1)} async-done(((bf16[192,3,5120]{0,1,2:T(4,128)(2,1)}), bf16[192,3,5120]{0,1,2:T(4,128)(2,1)}, u32[]{:S(2)}, u32[]{:S(2)}) %all-to-all-start) | async-done | bytes 5898272 | tf_op jit(solution)/shard_map/all_to_all | solution.py:45
  147.6 9.6 %all-to-all-start.1 = ((bf16[128,1,2,24,640]{4,3,2,1,0:T(8,128)(2,1)}), bf16[128,1,2,24,640]{4,3,2,1,0:T(8,128)(2,1)}, u32[]{:S(2)}, u32[]{:S(2)}) async-start(bf16[128,1,2,24,640]{4,3,2,1,0:T(8,128)(2,1)} %bitcast.97), calls=%async_computation.1 | async-start | bytes 15728640 | tf_op jit(solution)/shard_map/all_to_all | solution.py:64
  160.1 15.7 %copy.94 = bf16[192,3,8,640]{3,0,2,1:T(8,128)(2,1)} copy(bf16[192,3,8,640]{0,1,3,2:T(4,128)(2,1)} %bitcast.3) | data formatting | bytes 11796480 | tf_op jit(solution)/shard_map/all_to_all | solution.py:45
  175.8 5.1 fusion.50
  180.9 4.0 copy.85
  184.9 2.4 copy.87
  187.3 4.3 reshape.179
  193.5 62.9 %all-to-all-done.1 = bf16[128,1,2,24,640]{4,3,2,1,0:T(8,128)(2,1)} async-done(((bf16[128,1,2,24,640]{4,3,2,1,0:T(8,128)(2,1)}), bf16[128,1,2,24,640]{4,3,2,1,0:T(8,128)(2,1)}, u32[]{:S(2)}, u32[]{:S(2)}) %all-to-all-start.1) | async-done | bytes 7864352 | tf_op jit(solution)/shard_map/all_to_all | solution.py:64
  256.3 7.7 %copy.83 = bf16[16,1,2,8,24,640]{5,4,3,2,0,1:T(8,128)(2,1)} copy(bf16[16,1,2,8,24,640]{5,4,2,0,3,1:T(8,128)(2,1)} %bitcast.13) | data formatting | bytes 15728640 | tf_op jit(solution)/shard_map/transpose | solution.py:66
  264.0 8.0 %gather_fusion.1 = bf16[16,2,192,640]{3,2,1,0:T(8,128)(2,1)} fusion(bf16[16,2,192,640]{3,2,1,0:T(8,128)(2,1)} %bitcast.95, s32[1024]{0:T(1024)S(1)} %pad_clamp_fusion), kind=kCustom, calls=%fused_computation.1 | custom fusion | bytes 15728704 | tf_op jit(solution)/shard_map/gather | solution.py:82
  272.0 5.6 fusion.49
  277.6 8.5 %copy.84 = bf16[16,1,192,640]{2,0,3,1:T(8,128)(2,1)} copy(bf16[16,1,192,640]{3,2,1,0:T(8,128)(2,1)} %get-tuple-element.108) | data formatting | bytes 7864320 | tf_op jit(solution)/shard_map/slice | solution.py:84
  286.1 9.9 %reshape_squeeze.12 = bf16[3072,5,128]{0,2,1:T(8,128)(2,1)} reshape(bf16[16,1,192,640]{2,0,3,1:T(8,128)(2,1)} %copy.84) | data formatting | bytes 7864320 | tf_op jit(solution)/shard_map/reshape;squeeze | solution.py:84
  296.0 5.1 pad_maximum_fusion.1
  301.0 8.9 %copy.89 = bf16[4608,5,128]{2,0,1:T(8,128)(2,1)} copy(bf16[4608,5,128]{0,2,1:T(8,128)(2,1)} %pad_maximum_fusion.1) | data formatting | bytes 11796480
  309.9 8.5 %copy.86 = bf16[16,1,192,640]{2,0,3,1:T(8,128)(2,1)} copy(bf16[16,1,192,640]{3,2,1,0:T(8,128)(2,1)} %get-tuple-element.107) | data formatting | bytes 7864320 | tf_op jit(solution)/shard_map/slice | solution.py:85
  318.4 9.8 %reshape_squeeze.14 = bf16[3072,5,128]{0,2,1:T(8,128)(2,1)} reshape(bf16[16,1,192,640]{2,0,3,1:T(8,128)(2,1)} %copy.86) | data formatting | bytes 7864320 | tf_op jit(solution)/shard_map/reshape;squeeze | solution.py:85
  328.3 5.1 pad_maximum_fusion.2
  333.3 9.0 %copy.90 = bf16[4608,5,128]{2,0,1:T(8,128)(2,1)} copy(bf16[4608,5,128]{0,2,1:T(8,128)(2,1)} %pad_maximum_fusion.2) | data formatting | bytes 11796480
  342.3 214.1 %while.11 = (s32[]{:T(128)}, bf16[6,256,5,128]{3,1,2,0:T(8,128)(2,1)S(1)}, bf16[6,256,5,128]{3,1,2,0:T(8,128)(2,1)}, bf16[4608,5,128]{2,0,1:T(8,128)(2,1)}, bf16...) while((s32[]{:T(128)}, bf16[6,256,5,128]{3,1,2,0:T(8,128)(2,1)S(1)}, ...), condition=%wide.region_11.12_spmd.clone, body=%wide.region_8.11_spmd.clone.sunk | while | flops 3085118464 | bytes 106874992 | solution.py:95
  342.3 13.9 %fusion.66 = (f32[5,256]{1,0:T(8,128)S(1)}, f32[5,256,4608]{2,1,0:T(8,128)}) fusion(pred[4608]{0:T(1024)(128)(4,1)S(1)} %fusion.65, bf16[4608,5,128]{2,0,1:T(8,128)(2,1)} %get-tuple-element.178, bf16[6,256,5,128]{3,1,2,0:T(8,128)(2,1)} %get-tuple-element.177, s32[]{:T(128)} %get-tuple-element.168), kind=kOutput, calls=%fused_computation.5.clone.1 | convolution fusion | flops 1527642880 | bytes 29829120 | tf_op jit(solution)/shard_map/while/body/eval_jaxpr/qhd,khd->hqk/dot_general | solution.py:21
  356.2 10.9 %fusion.67 = f32[5,256]{1,0:T(8,128)S(1)} fusion(f32[5,256,4608]{2,1,0:T(8,128)} %get-tuple-element.159, f32[5,256]{1,0:T(8,128)S(1)} %get-tuple-element.160, pred[4608]{0:T(1024)(128)(4,1)S(1)} %fusion.65), kind=kLoop, calls=%fused_computation.6.clone.1 | loop fusion | flops 23591680 | bytes 23607808 | tf_op jit(solution)/shard_map/while/body/eval_jaxpr/reduce_sum | solution.py:27
  367.1 10.9 %fusion.68 = bf16[6,256,5,128]{3,1,2,0:T(8,128)(2,1)S(1)} fusion(bf16[6,256,5,128]{3,1,2,0:T(8,128)(2,1)S(1)} %get-tuple-element.169, s32[]{:T(128)} %get-tuple-element.168, bf16[4608,5,128]{2,0,1:T(8,128)(2,1)S(1)} %copy-done.5, f32[5,256,4608]{2,1,0:T(8,128)} %get-tuple-element.159, f32[5,256]{1,0:T(8,128)S(1)} %get-tuple-element.160, ...), kind=kOutput, calls=%fused_computation.14.clone.1 | convolution fusion | flops 1533870080 | bytes 29840388 | tf_op jit(solution)/shard_map/while/body/eval_jaxpr/hqk,khd->qhd/dot_general | solution.py:28
  378.0 13.8 %fusion.66 = (f32[5,256]{1,0:T(8,128)S(1)}, f32[5,256,4608]{2,1,0:T(8,128)}) fusion(pred[4608]{0:T(1024)(128)(4,1)S(1)} %fusion.65, bf16[4608,5,128]{2,0,1:T(8,128)(2,1)} %get-tuple-element.178, bf16[6,256,5,128]{3,1,2,0:T(8,128)(2,1)} %get-tuple-element.177, s32[]{:T(128)} %get-tuple-element.168), kind=kOutput, calls=%fused_computation.5.clone.1 | convolution fusion | flops 1527642880 | bytes 29829120 | tf_op jit(solution)/shard_map/while/body/eval_jaxpr/qhd,khd->hqk/dot_general | solution.py:21
  391.9 10.9 %fusion.67 = f32[5,256]{1,0:T(8,128)S(1)} fusion(f32[5,256,4608]{2,1,0:T(8,128)} %get-tuple-element.159, f32[5,256]{1,0:T(8,128)S(1)} %get-tuple-element.160, pred[4608]{0:T(1024)(128)(4,1)S(1)} %fusion.65), kind=kLoop, calls=%fused_computation.6.clone.1 | loop fusion | flops 23591680 | bytes 23607808 | tf_op jit(solution)/shard_map/while/body/eval_jaxpr/reduce_sum | solution.py:27
  402.8 10.9 %fusion.68 = bf16[6,256,5,128]{3,1,2,0:T(8,128)(2,1)S(1)} fusion(bf16[6,256,5,128]{3,1,2,0:T(8,128)(2,1)S(1)} %get-tuple-element.169, s32[]{:T(128)} %get-tuple-element.168, bf16[4608,5,128]{2,0,1:T(8,128)(2,1)S(1)} %copy-done.5, f32[5,256,4608]{2,1,0:T(8,128)} %get-tuple-element.159, f32[5,256]{1,0:T(8,128)S(1)} %get-tuple-element.160, ...), kind=kOutput, calls=%fused_computation.14.clone.1 | convolution fusion | flops 1533870080 | bytes 29840388 | tf_op jit(solution)/shard_map/while/body/eval_jaxpr/hqk,khd->qhd/dot_general | solution.py:28
  413.7 13.8 %fusion.66 = (f32[5,256]{1,0:T(8,128)S(1)}, f32[5,256,4608]{2,1,0:T(8,128)}) fusion(pred[4608]{0:T(1024)(128)(4,1)S(1)} %fusion.65, bf16[4608,5,128]{2,0,1:T(8,128)(2,1)} %get-tuple-element.178, bf16[6,256,5,128]{3,1,2,0:T(8,128)(2,1)} %get-tuple-element.177, s32[]{:T(128)} %get-tuple-element.168), kind=kOutput, calls=%fused_computation.5.clone.1 | convolution fusion | flops 1527642880 | bytes 29829120 | tf_op jit(solution)/shard_map/while/body/eval_jaxpr/qhd,khd->hqk/dot_general | solution.py:21
  427.6 10.9 %fusion.67 = f32[5,256]{1,0:T(8,128)S(1)} fusion(f32[5,256,4608]{2,1,0:T(8,128)} %get-tuple-element.159, f32[5,256]{1,0:T(8,128)S(1)} %get-tuple-element.160, pred[4608]{0:T(1024)(128)(4,1)S(1)} %fusion.65), kind=kLoop, calls=%fused_computation.6.clone.1 | loop fusion | flops 23591680 | bytes 23607808 | tf_op jit(solution)/shard_map/while/body/eval_jaxpr/reduce_sum | solution.py:27
  438.5 10.9 %fusion.68 = bf16[6,256,5,128]{3,1,2,0:T(8,128)(2,1)S(1)} fusion(bf16[6,256,5,128]{3,1,2,0:T(8,128)(2,1)S(1)} %get-tuple-element.169, s32[]{:T(128)} %get-tuple-element.168, bf16[4608,5,128]{2,0,1:T(8,128)(2,1)S(1)} %copy-done.5, f32[5,256,4608]{2,1,0:T(8,128)} %get-tuple-element.159, f32[5,256]{1,0:T(8,128)S(1)} %get-tuple-element.160, ...), kind=kOutput, calls=%fused_computation.14.clone.1 | convolution fusion | flops 1533870080 | bytes 29840388 | tf_op jit(solution)/shard_map/while/body/eval_jaxpr/hqk,khd->qhd/dot_general | solution.py:28
  449.4 13.8 %fusion.66 = (f32[5,256]{1,0:T(8,128)S(1)}, f32[5,256,4608]{2,1,0:T(8,128)}) fusion(pred[4608]{0:T(1024)(128)(4,1)S(1)} %fusion.65, bf16[4608,5,128]{2,0,1:T(8,128)(2,1)} %get-tuple-element.178, bf16[6,256,5,128]{3,1,2,0:T(8,128)(2,1)} %get-tuple-element.177, s32[]{:T(128)} %get-tuple-element.168), kind=kOutput, calls=%fused_computation.5.clone.1 | convolution fusion | flops 1527642880 | bytes 29829120 | tf_op jit(solution)/shard_map/while/body/eval_jaxpr/qhd,khd->hqk/dot_general | solution.py:21
  463.3 10.9 %fusion.67 = f32[5,256]{1,0:T(8,128)S(1)} fusion(f32[5,256,4608]{2,1,0:T(8,128)} %get-tuple-element.159, f32[5,256]{1,0:T(8,128)S(1)} %get-tuple-element.160, pred[4608]{0:T(1024)(128)(4,1)S(1)} %fusion.65), kind=kLoop, calls=%fused_computation.6.clone.1 | loop fusion | flops 23591680 | bytes 23607808 | tf_op jit(solution)/shard_map/while/body/eval_jaxpr/reduce_sum | solution.py:27
  474.2 10.9 %fusion.68 = bf16[6,256,5,128]{3,1,2,0:T(8,128)(2,1)S(1)} fusion(bf16[6,256,5,128]{3,1,2,0:T(8,128)(2,1)S(1)} %get-tuple-element.169, s32[]{:T(128)} %get-tuple-element.168, bf16[4608,5,128]{2,0,1:T(8,128)(2,1)S(1)} %copy-done.5, f32[5,256,4608]{2,1,0:T(8,128)} %get-tuple-element.159, f32[5,256]{1,0:T(8,128)S(1)} %get-tuple-element.160, ...), kind=kOutput, calls=%fused_computation.14.clone.1 | convolution fusion | flops 1533870080 | bytes 29840388 | tf_op jit(solution)/shard_map/while/body/eval_jaxpr/hqk,khd->qhd/dot_general | solution.py:28
  485.1 13.8 %fusion.66 = (f32[5,256]{1,0:T(8,128)S(1)}, f32[5,256,4608]{2,1,0:T(8,128)}) fusion(pred[4608]{0:T(1024)(128)(4,1)S(1)} %fusion.65, bf16[4608,5,128]{2,0,1:T(8,128)(2,1)} %get-tuple-element.178, bf16[6,256,5,128]{3,1,2,0:T(8,128)(2,1)} %get-tuple-element.177, s32[]{:T(128)} %get-tuple-element.168), kind=kOutput, calls=%fused_computation.5.clone.1 | convolution fusion | flops 1527642880 | bytes 29829120 | tf_op jit(solution)/shard_map/while/body/eval_jaxpr/qhd,khd->hqk/dot_general | solution.py:21
  498.9 10.9 %fusion.67 = f32[5,256]{1,0:T(8,128)S(1)} fusion(f32[5,256,4608]{2,1,0:T(8,128)} %get-tuple-element.159, f32[5,256]{1,0:T(8,128)S(1)} %get-tuple-element.160, pred[4608]{0:T(1024)(128)(4,1)S(1)} %fusion.65), kind=kLoop, calls=%fused_computation.6.clone.1 | loop fusion | flops 23591680 | bytes 23607808 | tf_op jit(solution)/shard_map/while/body/eval_jaxpr/reduce_sum | solution.py:27
  509.9 10.9 %fusion.68 = bf16[6,256,5,128]{3,1,2,0:T(8,128)(2,1)S(1)} fusion(bf16[6,256,5,128]{3,1,2,0:T(8,128)(2,1)S(1)} %get-tuple-element.169, s32[]{:T(128)} %get-tuple-element.168, bf16[4608,5,128]{2,0,1:T(8,128)(2,1)S(1)} %copy-done.5, f32[5,256,4608]{2,1,0:T(8,128)} %get-tuple-element.159, f32[5,256]{1,0:T(8,128)S(1)} %get-tuple-element.160, ...), kind=kOutput, calls=%fused_computation.14.clone.1 | convolution fusion | flops 1533870080 | bytes 29840388 | tf_op jit(solution)/shard_map/while/body/eval_jaxpr/hqk,khd->qhd/dot_general | solution.py:28
  520.8 13.8 %fusion.66 = (f32[5,256]{1,0:T(8,128)S(1)}, f32[5,256,4608]{2,1,0:T(8,128)}) fusion(pred[4608]{0:T(1024)(128)(4,1)S(1)} %fusion.65, bf16[4608,5,128]{2,0,1:T(8,128)(2,1)} %get-tuple-element.178, bf16[6,256,5,128]{3,1,2,0:T(8,128)(2,1)} %get-tuple-element.177, s32[]{:T(128)} %get-tuple-element.168), kind=kOutput, calls=%fused_computation.5.clone.1 | convolution fusion | flops 1527642880 | bytes 29829120 | tf_op jit(solution)/shard_map/while/body/eval_jaxpr/qhd,khd->hqk/dot_general | solution.py:21
  534.6 10.9 %fusion.67 = f32[5,256]{1,0:T(8,128)S(1)} fusion(f32[5,256,4608]{2,1,0:T(8,128)} %get-tuple-element.159, f32[5,256]{1,0:T(8,128)S(1)} %get-tuple-element.160, pred[4608]{0:T(1024)(128)(4,1)S(1)} %fusion.65), kind=kLoop, calls=%fused_computation.6.clone.1 | loop fusion | flops 23591680 | bytes 23607808 | tf_op jit(solution)/shard_map/while/body/eval_jaxpr/reduce_sum | solution.py:27
  545.6 10.9 %fusion.68 = bf16[6,256,5,128]{3,1,2,0:T(8,128)(2,1)S(1)} fusion(bf16[6,256,5,128]{3,1,2,0:T(8,128)(2,1)S(1)} %get-tuple-element.169, s32[]{:T(128)} %get-tuple-element.168, bf16[4608,5,128]{2,0,1:T(8,128)(2,1)S(1)} %copy-done.5, f32[5,256,4608]{2,1,0:T(8,128)} %get-tuple-element.159, f32[5,256]{1,0:T(8,128)S(1)} %get-tuple-element.160, ...), kind=kOutput, calls=%fused_computation.14.clone.1 | convolution fusion | flops 1533870080 | bytes 29840388 | tf_op jit(solution)/shard_map/while/body/eval_jaxpr/hqk,khd->qhd/dot_general | solution.py:28
  557.7 3.0 copy.91
  560.7 3.3 all_to_all.33
  564.0 31.6 %all_to_all.39 = bf16[8,192,640]{2,1,0:T(8,128)(2,1)S(1)} all-to-all(bf16[8,192,640]{2,1,0:T(8,128)(2,1)} %all_to_all.33), channel_id=1, replica_groups=mesh['wide'=8,'rep'=16] {'wide'}, dimensions={0} | all-to-all | bytes 3932160 | tf_op jit(solution)/shard_map/all_to_all | solution.py:97
  (58 shorter events, 12.3 us)
Async XLA Ops:
  0.0 31.3 %copy-start = (s32[16,16]{1,0:T(8,128)S(1)}, s32[16,16]{1,0:T(8,128)}, u32[]{:S(2)}) copy-start(s32[16,16]{1,0:T(8,128)} %param.12) | copy-start | bytes 3076
  0.0 4.9 copy-start.2
  0.0 4.8 copy-start.8
  24.8 6.5 %copy-start.9 = (s32[16]{0:T(128)S(1)}, s32[16]{0:T(128)}, u32[]{:S(2)}) copy-start(s32[16]{0:T(128)} %param.13) | copy-start | bytes 196
  24.8 122.7 %all-to-all-start = ((bf16[192,3,5120]{0,1,2:T(4,128)(2,1)}), bf16[192,3,5120]{0,1,2:T(4,128)(2,1)}, u32[]{:S(2)}, u32[]{:S(2)}) async-start(bf16[192,3,5120]{0,1,2:T(4,128)(2,1)} %copy.77), calls=%async_computation | async-start | bytes 20971520 | tf_op jit(solution)/shard_map/all_to_all | solution.py:45
  147.6 10.3 %copy-start.10 = (s32[16]{0:T(128)S(1)}, s32[16]{0:T(128)}, u32[]{:S(2)}) copy-start(s32[16]{0:T(128)} %param.11) | copy-start | bytes 196
  147.6 108.7 %all-to-all-start.1 = ((bf16[128,1,2,24,640]{4,3,2,1,0:T(8,128)(2,1)}), bf16[128,1,2,24,640]{4,3,2,1,0:T(8,128)(2,1)}, u32[]{:S(2)}, u32[]{:S(2)}) async-start(bf16[128,1,2,24,640]{4,3,2,1,0:T(8,128)(2,1)} %bitcast.97), calls=%async_computation.1 | async-start | bytes 15728640 | tf_op jit(solution)/shard_map/all_to_all | solution.py:64
  286.1 9.9 %copy-start.4 = (bf16[1536,1,640]{0,2,1:T(8,128)(2,1)S(1)}, bf16[1536,1,640]{0,2,1:T(8,128)(2,1)}, u32[]{:S(2)}) copy-start(bf16[1536,1,640]{0,2,1:T(8,128)(2,1)} %copy.85) | copy-start | bytes 5898244
  318.4 9.8 %copy-start.3 = (bf16[1536,1,640]{0,2,1:T(8,128)(2,1)S(1)}, bf16[1536,1,640]{0,2,1:T(8,128)(2,1)}, u32[]{:S(2)}) copy-start(bf16[1536,1,640]{0,2,1:T(8,128)(2,1)} %copy.87) | copy-start | bytes 5898244
  333.3 9.0 %copy-start.6 = (bf16[6,256,5,128]{3,1,2,0:T(8,128)(2,1)S(1)}, bf16[6,256,5,128]{3,1,2,0:T(8,128)(2,1)}, u32[]{:S(2)}) copy-start(bf16[6,256,5,128]{3,1,2,0:T(8,128)(2,1)} %custom-call.4) | copy-start | bytes 5898244
  356.2 10.9 %copy-start.5 = (bf16[4608,5,128]{2,0,1:T(8,128)(2,1)S(1)}, bf16[4608,5,128]{2,0,1:T(8,128)(2,1)}, u32[]{:S(2)}) copy-start(bf16[4608,5,128]{2,0,1:T(8,128)(2,1)} %get-tuple-element.179) | copy-start | bytes 17694724 | tf_op jit(solution)/shard_map/while
  391.9 10.9 %copy-start.5 = (bf16[4608,5,128]{2,0,1:T(8,128)(2,1)S(1)}, bf16[4608,5,128]{2,0,1:T(8,128)(2,1)}, u32[]{:S(2)}) copy-start(bf16[4608,5,128]{2,0,1:T(8,128)(2,1)} %get-tuple-element.179) | copy-start | bytes 17694724 | tf_op jit(solution)/shard_map/while
  427.6 10.9 %copy-start.5 = (bf16[4608,5,128]{2,0,1:T(8,128)(2,1)S(1)}, bf16[4608,5,128]{2,0,1:T(8,128)(2,1)}, u32[]{:S(2)}) copy-start(bf16[4608,5,128]{2,0,1:T(8,128)(2,1)} %get-tuple-element.179) | copy-start | bytes 17694724 | tf_op jit(solution)/shard_map/while
  463.3 10.9 %copy-start.5 = (bf16[4608,5,128]{2,0,1:T(8,128)(2,1)S(1)}, bf16[4608,5,128]{2,0,1:T(8,128)(2,1)}, u32[]{:S(2)}) copy-start(bf16[4608,5,128]{2,0,1:T(8,128)(2,1)} %get-tuple-element.179) | copy-start | bytes 17694724 | tf_op jit(solution)/shard_map/while
  498.9 10.9 %copy-start.5 = (bf16[4608,5,128]{2,0,1:T(8,128)(2,1)S(1)}, bf16[4608,5,128]{2,0,1:T(8,128)(2,1)}, u32[]{:S(2)}) copy-start(bf16[4608,5,128]{2,0,1:T(8,128)(2,1)} %get-tuple-element.179) | copy-start | bytes 17694724 | tf_op jit(solution)/shard_map/while
  534.6 10.9 %copy-start.5 = (bf16[4608,5,128]{2,0,1:T(8,128)(2,1)S(1)}, bf16[4608,5,128]{2,0,1:T(8,128)(2,1)}, u32[]{:S(2)}) copy-start(bf16[4608,5,128]{2,0,1:T(8,128)(2,1)} %get-tuple-element.179) | copy-start | bytes 17694724 | tf_op jit(solution)/shard_map/while
  556.5 1.3 copy-start.7
  560.7 38.3 %copy-start.1 = (s32[16,16]{1,0:T(8,128)S(1)}, s32[16,16]{1,0:T(8,128)}, u32[]{:S(2)}) copy-start(s32[16,16]{1,0:T(8,128)} %param.12) | copy-start | bytes 3076
where the time goes:
time: 602 us; the launch traced here: 599 us
  waiting for transfers between devices  161 us (27%)
  local copies, waits for them, and re-layouts  155 us (26%)
  matrix products  148 us (25%)
  other arithmetic  85.8 us (14%)
  blocking collectives  31.6 us (5%)
  starting transfers between devices  16.1 us (3%)
    all_to_all x1, waiting for transfers between devices, body(): lax.all_to_all(framed, 'wide', split_axis=2, concat_axis=0, tiled=True)  98.5 us
    dot_general x6, matrix products, attend_block(): jnp.einsum('qhd,khd->hqk', query_rows, all_keys, preferred_element_type=j...  83.1 us
    reduce_sum x6, other arithmetic, attend_block(): row_total = jnp.sum(weights, axis=-1, keepdims=True)  65.6 us
    dot_general x6, matrix products, attend_block(): jnp.einsum('hqk,khd->qhd', weights.astype(jnp.bfloat16), all_values, pref...  65.1 us
    all_to_all x1, waiting for transfers between devices, body(): lax.all_to_all(moved, ('wide', 'rep'), split_axis=0, concat_axis=0, tiled...  62.9 us
    all_to_all x1, blocking collectives, body(): lax.all_to_all(attended, 'wide', split_axis=0, concat_axis=1, tiled=True)  31.6 us
    unnamed x24, local copies, waits for them, and re-layouts  26 us
    all_to_all x1, local copies, waits for them, and re-layouts, body(): lax.all_to_all(framed, 'wide', split_axis=2, concat_axis=0, tiled=True)  15.7 us
  transfers between devices with their start and end apart: 2, of which 2 were waited for; matrix products, arithmetic and copies ran while one was open for 9% of the time, Pallas kernels for 0%

commit v1 on v0

v1 whole, which is shorter than its diff:
```python
import functools
import math

import jax
import jax.numpy as jnp
from jax import lax
from jax.experimental import pallas as pl
from jax.experimental.pallas import tpu as pltpu
from jax.sharding import PartitionSpec as P

MESH = pl.DeviceIdType.MESH
HD = 128
HEADS_CHUNK = 4
SLOTS = 3
CHUNK = HD * HEADS_CHUNK
EPSILON = 1e-06
SCALE = math.log2(math.e) / math.sqrt(HD)
ORDER = ((1, 0), (0, 1), (3, 2), (2, 3), (3, 0), (0, 3), (1, 2), (2, 1), (2, 0), (0, 2), (1, 1), (3, 3), (1, 3), (3, 1), (2, 2))


def lanes(start, size):
    return pl.ds(pl.multiple_of(start, 128), size)


def kernel(
    sel_ref, vis_ref, qkv_ref, gains_ref, cache_ref, out_ref,
    qk, raw_even, raw_odd, gathered, arrived, queries, keys_new, values_new, keys, values, partial, relay_in, final_in,
    stats_col, stats, relay_stats, final_stats, weights_row,
    load_sem, raw_sem, own_sem, cache_send, cache_recv, first_send, first_recv, hop_send, hop_recv,
    kv_send, kv_recv, s1_send, s1_recv, s2_send, s2_recv, out_send, out_recv, out_own,
):
    wide, rep = lax.axis_index("wide"), lax.axis_index("rep")
    x, core = wide // 2, wide % 2
    y, z = rep // 4, rep % 4
    other = 1 - core
    right, left = (x + 1) % 4, (x + 3) % 4
    chunks, rows_all, _ = queries.shape
    tokens = qk.shape[1]
    quarter = 2 * tokens
    half_width = chunks * CHUNK
    groups = sel_ref.shape[0]
    raws = (raw_even, raw_odd)

    def remote(src, dst, send, recv, to_wide, to_rep):
        return pltpu.make_async_remote_copy(
            src_ref=src, dst_ref=dst, send_sem=send, recv_sem=recv, device_id=(to_wide, to_rep), device_id_type=MESH
        )

    def group_at(k):
        dy, dz = ORDER[k]
        sign = 1 - 2 * core
        return ((y + dy * sign + 4) % 4) * 4 + (z + dz * sign + 4) % 4

    def cache_copies(j):
        copies = []
        for k in range(len(ORDER)):
            to = group_at(k)
            for h in range(2):
                copies.append(remote(
                    gathered.at[j % SLOTS, to, h], arrived.at[j, rep, core], cache_send.at[j, 2 * k + h],
                    cache_recv.at[j, rep * 2 + core], 2 * x + h, to))
        copies.append(remote(
            gathered.at[j % SLOTS, rep, other], arrived.at[j, rep, core], cache_send.at[j, 2 * len(ORDER)],
            cache_recv.at[j, rep * 2 + core], 2 * x + other, rep))
        return copies

    def wait_cache(j):
        for k in range(len(ORDER)):
            owner = group_at(k)
            for h in range(2):
                remote(gathered.at[0, 0, 0], arrived.at[j, owner, h], cache_send.at[j, 0],
                       cache_recv.at[j, owner * 2 + h], wide, rep).wait_recv()
        remote(gathered.at[0, 0, 0], arrived.at[j, rep, other], cache_send.at[j, 0],
               cache_recv.at[j, rep * 2 + other], wide, rep).wait_recv()

    def piece(j, position):
        return queries.at[j, pl.ds(pl.multiple_of(position * tokens, 16), tokens)]

    def own_columns(h, j):
        return lanes(h * half_width + j * CHUNK, CHUNK)

    def first_copies(j):
        copies = [remote(qk.at[0, :, own_columns(other, j)], piece(j, wide), first_send.at[j, 0], first_recv.at[j, 0],
                         2 * x + other, rep)]
        for side, to in enumerate((right, left)):
            for h in range(2):
                copies.append(remote(
                    qk.at[0, :, own_columns(h, j)], piece(j, wide), first_send.at[j, 1 + 2 * side + h],
                    first_recv.at[j, 1 + 2 * side + core], 2 * to + h, rep))
        return copies

    def wait_first(j):
        sources = [2 * x + other, 2 * left, 2 * left + 1, 2 * right, 2 * right + 1]
        for slot, source in enumerate(sources):
            remote(piece(j, wide), piece(j, source), first_send.at[j, 0], first_recv.at[j, slot], wide, rep).wait_recv()

    def hop_copies(j):
        return [
            remote(piece(j, 2 * left), piece(j, 2 * left), hop_send.at[j, 0], hop_recv.at[j, 0], 2 * right + core, rep),
            remote(piece(j, 2 * right + 1), piece(j, 2 * right + 1), hop_send.at[j, 1], hop_recv.at[j, 1], 2 * left + core, rep),
        ]

    def wait_hop(j):
        far = (x + 2) % 4
        for slot in range(2):
            remote(piece(j, wide), piece(j, 2 * far + slot), hop_send.at[j, 0], hop_recv.at[j, slot], wide, rep).wait_recv()

    def token_rows(c):
        return pl.ds(pl.multiple_of(c * tokens, 16), tokens)

    def kv_copies(j):
        return [
            remote(qk.at[1, :, own_columns(other, j)], keys_new.at[j, token_rows(core)], kv_send.at[j, 0], kv_recv.at[j, 0],
                   2 * x + other, rep),
            remote(qkv_ref.at[2, :, own_columns(other, j)], values_new.at[j, token_rows(core)], kv_send.at[j, 1],
                   kv_recv.at[j, 1], 2 * x + other, rep),
        ]

    def wait_kv(j):
        remote(keys_new.at[j, token_rows(core)], keys_new.at[j, token_rows(other)], kv_send.at[j, 0], kv_recv.at[j, 0],
               wide, rep).wait_recv()
        remote(keys_new.at[j, token_rows(core)], values_new.at[j, token_rows(other)], kv_send.at[j, 1], kv_recv.at[j, 1],
               wide, rep).wait_recv()

    def own_copies(j):
        return [
            pltpu.make_async_copy(qk.at[0, :, own_columns(core, j)], piece(j, wide), own_sem.at[j, 0]),
            pltpu.make_async_copy(qk.at[1, :, own_columns(core, j)], keys_new.at[j, token_rows(core)], own_sem.at[j, 1]),
            pltpu.make_async_copy(qkv_ref.at[2, :, own_columns(core, j)], values_new.at[j, token_rows(core)], own_sem.at[j, 2]),
        ]

    def raw_copies(j):
        return [
            pltpu.make_async_copy(cache_ref.at[:, :, :, :, own_columns(h, j)], raws[j % 2].at[h], raw_sem.at[j % 2, h])
            for h in range(2)
        ]

    def gather(j):
        for copy in raw_copies(j):
            copy.wait()

        def place(to, carry):
            row = sel_ref[to]
            for h in range(2):
                gathered[j % SLOTS, to, h] = raws[j % 2][h, row]
            return carry

        lax.fori_loop(0, groups, place, 0)
        arrived[j, rep, core] = raws[j % 2][core, sel_ref[rep]]

        if j + 2 < chunks:
            start(raw_copies(j + 2))

    def normalize(which):
        def rows_step(i, carry):
            block = pl.ds(pl.multiple_of(i * 16, 16), 16)
            widened = qk[which, block, :].astype(jnp.float32)
            mean_square = jnp.mean(widened * widened, axis=-1, keepdims=True)
            scaled = widened * lax.rsqrt(mean_square + EPSILON) * gains_ref[which : which + 1, :]
            qk[which, block, :] = scaled.astype(jnp.bfloat16)
            return carry

        lax.fori_loop(0, tokens // 16, rows_step, 0)

    def start(copies):
        for copy in copies:
            copy.start()

    def quarter_rows(d):
        return pl.ds(pl.multiple_of(d * quarter, 16), quarter)

    def half_rows(d, part):
        return pl.ds(pl.multiple_of(d * quarter + part * tokens, 16), tokens)

    def s1_copies(j):
        far = (x + 2) % 4
        copies = []
        for slot, to in enumerate((right, left)):
            copies.append(remote(partial.at[j, half_rows(far, 1 - slot)], relay_in.at[j, slot], s1_send.at[j, 2 * slot],
                                 s1_recv.at[j, 2 * slot], 2 * to + core, rep))
            copies.append(remote(stats.at[j, far], relay_stats.at[j, slot], s1_send.at[j, 2 * slot + 1],
                                 s1_recv.at[j, 2 * slot + 1], 2 * to + core, rep))
        return copies

    def s2_copies(j, slot):
        to = (right, left)[slot]
        return [
            remote(partial.at[j, quarter_rows(to)], final_in.at[j, slot], s2_send.at[j, 2 * slot], s2_recv.at[j, 2 * slot],
                   2 * to + core, rep),
            remote(stats.at[j, to], final_stats.at[j, slot], s2_send.at[j, 2 * slot + 1], s2_recv.at[j, 2 * slot + 1],
                   2 * to + core, rep),
        ]

    def forward_partial(j):
        for slot, to in enumerate((right, left)):
            remote(relay_in.at[j, slot], relay_in.at[j, slot], s1_send.at[j, 0], s1_recv.at[j, 2 * slot], wide, rep).wait_recv()
            remote(relay_stats.at[j, slot], relay_stats.at[j, slot], s1_send.at[j, 0], s1_recv.at[j, 2 * slot + 1], wide,
                   rep).wait_recv()
            here, came = stats[j, to], relay_stats[j, slot]
            top = jnp.maximum(here, came)
            a, b = jnp.exp2(here - top), jnp.exp2(came - top)
            total = a + b
            token = lax.broadcasted_iota(jnp.int32, here.shape, 1)
            merged = token >= tokens if slot == 0 else token < tokens
            stats[j, to] = jnp.where(merged, top + jnp.log2(total), here)
            weights_row[0:8] = a / total
            weights_row[8:16] = b / total
            part = 1 - slot
            columns = jnp.transpose(weights_row[...])[part * tokens : (part + 1) * tokens]
            place = half_rows(to, part)
            for h in range(HEADS_CHUNK):
                feature = slice(h * HD, (h + 1) * HD)
                mixed = columns[:, h : h + 1] * partial[j, place, feature].astype(jnp.float32)
                mixed += columns[:, 8 + h : 9 + h] * relay_in[j, slot, :, feature].astype(jnp.float32)
                partial[j, place, feature] = mixed.astype(jnp.bfloat16)
            start(s2_copies(j, slot))

    def out_copies(j):
        place = own_columns(core, j)
        return (
            remote(partial.at[j, half_rows(x, other)], out_ref.at[:, place], out_send.at[j], out_recv.at[j], 2 * x + other, rep),
            pltpu.make_async_copy(partial.at[j, half_rows(x, core)], out_ref.at[:, place], out_own.at[j]),
        )

    def finish(j):
        for slot in range(2):
            remote(final_in.at[j, slot], final_in.at[j, slot], s2_send.at[j, 0], s2_recv.at[j, 2 * slot], wide, rep).wait_recv()
            remote(final_stats.at[j, slot], final_stats.at[j, slot], s2_send.at[j, 0], s2_recv.at[j, 2 * slot + 1], wide,
                   rep).wait_recv()
        here, first, second = stats[j, x], final_stats[j, 0], final_stats[j, 1]
        top = jnp.maximum(here, jnp.maximum(first, second))
        a, b, c = jnp.exp2(here - top), jnp.exp2(first - top), jnp.exp2(second - top)
        total = a + b + c
        weights_row[0:8] = a / total
        weights_row[8:16] = b / total
        weights_row[16:24] = c / total
        columns = jnp.transpose(weights_row[...])
        place = quarter_rows(x)
        for h in range(HEADS_CHUNK):
            feature = slice(h * HD, (h + 1) * HD)
            mixed = columns[:, h : h + 1] * partial[j, place, feature].astype(jnp.float32)
            mixed += columns[:, 8 + h : 9 + h] * final_in[j, 0, :, feature].astype(jnp.float32)
            mixed += columns[:, 16 + h : 17 + h] * final_in[j, 1, :, feature].astype(jnp.float32)
            partial[j, place, feature] = mixed.astype(jnp.bfloat16)
        start(out_copies(j))

    def prepare(j):
        keys[0:quarter] = keys_new[j]
        for h in range(HEADS_CHUNK):
            values[h, 0:quarter, 0:HD] = values_new[j, :, h * HD : (h + 1) * HD]
        rows = quarter // 8

        def block(owner, carry):
            seen = vis_ref[owner]
            count = 2 * 24
            here = pl.ds(pl.multiple_of(quarter + owner * count, 16), count)
            spare = keys_new[j, 0:count].astype(jnp.float32)
            k = arrived[j, owner, :, 0].astype(jnp.float32).reshape(count, CHUNK)
            v = arrived[j, owner, :, 1].astype(jnp.float32).reshape(count, CHUNK)
            keys[here] = (k * seen + spare * (1.0 - seen)).astype(jnp.bfloat16)
            v = (v * seen).astype(jnp.bfloat16)
            for h in range(HEADS_CHUNK):
                values[h, here, 0:HD] = v[:, h * HD : (h + 1) * HD]
            return carry

        lax.fori_loop(0, groups, block, 0)

    def attend(j, h):
        feature = lanes(h * HD, HD)
        tile = rows_all // 2
        k = keys[:, feature]
        lane = lax.broadcasted_iota(jnp.int32, (tile, 128), 1)
        for part in range(2):
            place = slice(part * tile, (part + 1) * tile)
            q = queries[j, place, feature]
            scores = lax.dot_general(q, k, (((1,), (1,)), ((), ())), preferred_element_type=jnp.float32)
            row_max = jnp.max(scores, axis=1, keepdims=True) * SCALE
            weights = jnp.exp2(scores * SCALE - row_max)
            mixed = jnp.dot(weights.astype(jnp.bfloat16), values[h], preferred_element_type=jnp.float32)
            total = mixed[:, HD:]
            partial[j, place, feature] = (mixed[:, :HD] / total).astype(jnp.bfloat16)
            stats_col[place, :] = jnp.where(lane == h, row_max + jnp.log2(total), stats_col[place, :])

    barrier = pltpu.get_barrier_semaphore()
    peers = [(2 * x + h, group_at(k)) for k in range(len(ORDER)) for h in range(2)]
    peers += [(2 * x + other, rep)] + [(2 * to + h, rep) for to in (right, left) for h in range(2)]
    for peer in peers:
        pl.semaphore_signal(barrier, inc=1, device_id=peer, device_id_type=MESH)
    loads = [pltpu.make_async_copy(qkv_ref.at[i], qk.at[i], load_sem.at[i]) for i in range(2)]
    loads[0].start()
    start(raw_copies(0))
    loads[1].start()
    start(raw_copies(1))
    for h in range(HEADS_CHUNK):
        values[h, 0:quarter, HD:] = jnp.ones((quarter, HD), jnp.bfloat16)

    def shares(owner, carry):
        count = 2 * 24
        here = pl.ds(pl.multiple_of(quarter + owner * count, 16), count)
        filled = jnp.full((count, HD), vis_ref[owner], jnp.float32).astype(jnp.bfloat16)
        for h in range(HEADS_CHUNK):
            values[h, here, HD:] = filled
        return carry

    lax.fori_loop(0, groups, shares, 0)
    stats_col[...] = jnp.zeros_like(stats_col)
    weights_row[...] = jnp.zeros_like(weights_row)
    gather(0)
    loads[0].wait()
    normalize(0)
    pl.semaphore_wait(barrier, len(peers))
    start(cache_copies(0))
    start(first_copies(0))
    gather(1)
    start(cache_copies(1))
    start(first_copies(1))
    loads[1].wait()
    normalize(1)

    def spread(j, carry):
        start(own_copies(j))
        start(kv_copies(j))
        return carry

    lax.fori_loop(0, chunks, spread, 0)

    for j in range(2, SLOTS):
        gather(j)
        start(cache_copies(j))
    wait_first(0)
    start(hop_copies(0))
    start(first_copies(2))

    def step(j, carry):
        @pl.when(j >= 1)
        def _():
            forward_partial(j - 1)

        wait_hop(j)
        wait_kv(j)
        for copy in own_copies(j):
            copy.wait()
        wait_cache(j)
        prepare(j)
        attend(j, 0)

        @pl.when(j + 1 < chunks)
        def _():
            wait_first(j + 1)
            start(hop_copies(j + 1))

        @pl.when(j + 3 < chunks)
        def _():
            start(first_copies(j + 3))

        for early in range(chunks - SLOTS):

            @pl.when(j == early)
            def _():
                for copy in cache_copies(early):
                    copy.wait_send()
                gather(early + SLOTS)
                start(cache_copies(early + SLOTS))

        def rest(h, inner):
            attend(j, h)
            return inner

        lax.fori_loop(1, HEADS_CHUNK, rest, 0)
        for d in range(4):
            stats[j, d] = jnp.transpose(stats_col[d * quarter : (d + 1) * quarter, :])[0:8]
        start(s1_copies(j))

        @pl.when(j >= 1)
        def _():
            finish(j - 1)

        return carry

    lax.fori_loop(0, chunks, step, 0)
    forward_partial(chunks - 1)
    finish(chunks - 1)

    def drain(j, carry):
        @pl.when(j + SLOTS >= chunks)
        def _():
            for copy in cache_copies(j):
                copy.wait_send()

        for copy in first_copies(j) + hop_copies(j) + kv_copies(j) + s1_copies(j) + s2_copies(j, 0) + s2_copies(j, 1):
            copy.wait_send()
        sent, kept = out_copies(j)
        sent.wait_send()
        sent.wait_recv()
        kept.wait()
        return carry

    lax.fori_loop(0, chunks, drain, 0)


def body(stretch_qkv, norm_gains, cache, cached_stretches, block_slot, video_of_group):
    rep = lax.axis_index("rep")
    groups = lax.axis_size("rep")
    _, tokens, _, width = stretch_qkv.shape
    slots = cache.shape[0]
    blocks = block_slot.shape[1]
    stretch = tokens * lax.axis_size("wide")
    block_len = cache.shape[2] * lax.axis_size("wide")
    videos = cached_stretches.shape[0]
    chunks = width // 2 // CHUNK
    picked = video_of_group[:, None] == jnp.arange(videos, dtype=jnp.int32)[None, :]
    table = jnp.sum(jnp.where(picked[:, :, None], block_slot[None], 0), axis=1)
    sel = jnp.sum(jnp.where(table // slots == rep, table % slots, 0), axis=1)
    mine = jnp.arange(groups, dtype=jnp.int32) == rep
    own_table = jnp.sum(jnp.where(mine[:, None], table, 0), axis=0)
    own_count = jnp.sum(jnp.where(mine[:, None] & picked, cached_stretches[None, :], 0))
    seen = jnp.arange(blocks, dtype=jnp.int32) * block_len < own_count * stretch
    from_owner = own_table[None, :] // slots == jnp.arange(groups, dtype=jnp.int32)[:, None]
    vis = jnp.sum(jnp.where(from_owner & seen[None, :], 1.0, 0.0), axis=1)

    bf16, f32 = jnp.bfloat16, jnp.float32
    rows_all = stretch
    quarter = 2 * tokens
    keys_count = quarter + groups * 2 * cache.shape[2]
    vmem, dma = pltpu.VMEM, pltpu.SemaphoreType.DMA
    peers = 2 * len(ORDER) + 1
    smem_spec = pl.BlockSpec(memory_space=pltpu.SMEM)
    any_spec = pl.BlockSpec(memory_space=pl.ANY)
    out = pl.pallas_call(
        kernel,
        name="attend_exchange",
        out_shape=jax.ShapeDtypeStruct((tokens, width), bf16),
        in_specs=[smem_spec, smem_spec, any_spec, pl.BlockSpec(memory_space=vmem), any_spec],
        out_specs=any_spec,
        scratch_shapes=[
            vmem((2, tokens, width), bf16),
            vmem((2, slots, 2, 3, 8, CHUNK), bf16),
            vmem((2, slots, 2, 3, 8, CHUNK), bf16),
            vmem((SLOTS, groups, 2, 2, 3, 8, CHUNK), bf16),
            vmem((chunks, groups, 2, 2, 3, 8, CHUNK), bf16),
            vmem((chunks, rows_all, CHUNK), bf16),
            vmem((chunks, quarter, CHUNK), bf16),
            vmem((chunks, quarter, CHUNK), bf16),
            vmem((keys_count, CHUNK), bf16),
            vmem((HEADS_CHUNK, keys_count, 2 * HD), bf16),
            vmem((chunks, rows_all, CHUNK), bf16),
            vmem((chunks, 2, tokens, CHUNK), bf16),
            vmem((chunks, 2, quarter, CHUNK), bf16),
            vmem((rows_all, 128), f32),
            vmem((chunks, 4, 8, quarter), f32),
            vmem((chunks, 2, 8, quarter), f32),
            vmem((chunks, 2, 8, quarter), f32),
            vmem((128, quarter), f32),
            dma((2,)),
            dma((2, 2)),
            dma((chunks, 3)),
            dma((chunks, peers)),
            dma((chunks, 2 * groups)),
            dma((chunks, 5)),
            dma((chunks, 5)),
            dma((chunks, 2)),
            dma((chunks, 2)),
            dma((chunks, 2)),
            dma((chunks, 2)),
            dma((chunks, 4)),
            dma((chunks, 4)),
            dma((chunks, 4)),
            dma((chunks, 4)),
            dma((chunks,)),
            dma((chunks,)),
            dma((chunks,)),
        ],
        compiler_params=pltpu.CompilerParams(collective_id=0, has_side_effects=True, vmem_limit_bytes=67043328),
    )(sel, vis, jnp.transpose(stretch_qkv[0], (1, 0, 2)), norm_gains, cache.reshape(slots, 2, 3, 8, width))
    return out[None]


def solution(mesh):
    in_specs = (P("rep", "wide", None, None), P(), P("rep", None, "wide", None), P(), P(), P())
    out_specs = P("rep", "wide", None)
    return jax.shard_map(body, mesh=mesh, in_specs=in_specs, out_specs=out_specs, check_vma=False)
```

time: 602 us -> 164 us (0.27)
  waiting for transfers between devices: 161 us -> 0 us
  Pallas kernels: 0 us -> 157 us
  local copies, waits for them, and re-layouts: 155 us -> 2.94 us
  matrix products: 148 us -> 0 us
  other arithmetic: 85.8 us -> 3.68 us
  blocking collectives: 31.6 us -> 0 us
  starting transfers between devices: 16.1 us -> 0 us
    all_to_all x2 -> x0, waiting for transfers between devices: 161 us -> none  [the longest x1 98.5 us: body(): lax.all_to_all(framed, 'wide', split_axis=2, concat_axis=0, tiled=True)]
    pallas_call x0 -> x1, Pallas kernels: none -> 157 us  [body(): pl.pallas_call(kernel, name='attend_exchange', out_shape=jax.ShapeDtypeSt...]
    dot_general x13 -> x0, matrix products: 148 us -> none  [the longest x6 83.1 us: attend_block(): jnp.einsum('qhd,khd->hqk', query_rows, all_keys, preferred_element_type=j...]
    reduce_sum x11 -> x3, other arithmetic: 71.1 us -> 2.93 us  [the longest x1 1.47 us: body(): own_table = jnp.sum(jnp.where(mine[:, None], table, 0), axis=0)]
    another operation x4 -> x0, local copies, waits for them, and re-layouts: 39.6 us -> none  [the longest x1 15.6 us: body(): framed = jnp.stack([queries, keys_new, stretch_rows[:, 2]], axis=1)]
    slice x8 -> x0, local copies, waits for them, and re-layouts: 35.9 us -> none  [the longest x2 14.1 us: body(): hist_values = history[:, 1].reshape(hist_span, heads_dev, HD)]
    all_to_all x1 -> x0, blocking collectives: 31.6 us -> none  [body(): lax.all_to_all(attended, 'wide', split_axis=0, concat_axis=1, tiled=True)]
    unnamed x24 -> x1, local copies, waits for them, and re-layouts: 26 us -> 2.94 us
  transfers between devices with their start and end apart: 2 -> 0, of which waited for: 2 -> 0; matrix products, arithmetic and copies ran while one was open for 9% -> 0% of each run, Pallas kernels for 0% -> 0%
where the time goes in v1:
time: 164 us
  Pallas kernels  157 us (96%)
  other arithmetic  3.68 us (2%)
  local copies, waits for them, and re-layouts  2.94 us (2%)
    pallas_call x1, Pallas kernels, body(): pl.pallas_call(kernel, name='attend_exchange', out_shape=jax.ShapeDtypeSt...  157 us

profile of v1, /device:TPU:1, one launch (start us, length us, event | category | flops | bytes accessed | tf_op | source)
XLA Modules:
  0.0 164.2 jit_solution(10092145060074581693)
XLA Ops:
  0.0 0.7 iota_compare_fusion.1
  0.7 0.8 select_reduce_fusion
  1.6 1.5 select_reduce_fusion.3
  3.7 0.7 select_reduce_fusion.1.vis_ref
  4.4 156.8 %attend_exchange.1 = bf16[192,5120]{1,0:T(8,128)(2,1)} custom-call(s32[16]{0:T(128)} %get-tuple-element.6.sel_ref, f32[16]{0:T(128)} %select_reduce_fusion.1.vis_ref, bf16[3,192,5120]{2,1,0:T(8,128)(2,1)} %bitcast.7, f32[2,5120]{1,0:T(2,128)} %gains_ref.1, bf16[16,2,3,8,5120]{4,3,2,1,0:T(8,128)(2,1)} %bitcast.5), custom_call_target="tpu_custom_call" | custom-call | tf_op jit(solution)/shard_map/attend_exchange/pallas_call | solution.py:429
  161.2 2.9 %copy.8 = bf16[1,192,5120]{2,1,0:T(8,128)(2,1)} copy(bf16[1,192,5120]{2,1,0:T(8,128)(2,1)} %bitcast.6) | data formatting | bytes 3932160
  (3 shorter events, 0.0 us)

commit v2 on v1

--- a/solution.py
+++ b/solution.py
@@ -23,9 +23,9 @@
 
 
 def kernel(
-    sel_ref, vis_ref, qkv_ref, gains_ref, cache_ref, out_ref,
+    counts_ref, slot_ref, video_ref, qkv_ref, gains_ref, cache_ref, out_ref,
     qk, raw_even, raw_odd, gathered, arrived, queries, keys_new, values_new, keys, values, partial, relay_in, final_in,
-    stats_col, stats, relay_stats, final_stats, weights_row,
+    stats_col, stats, relay_stats, final_stats, weights_row, sel_ref, vis_ref,
     load_sem, raw_sem, own_sem, cache_send, cache_recv, first_send, first_recv, hop_send, hop_recv,
     kv_send, kv_recv, s1_send, s1_recv, s2_send, s2_recv, out_send, out_recv, out_own,
 ):
@@ -38,7 +38,8 @@
     tokens = qk.shape[1]
     quarter = 2 * tokens
     half_width = chunks * CHUNK
-    groups = sel_ref.shape[0]
+    groups, blocks = slot_ref.shape
+    rows_held = cache_ref.shape[0]
     raws = (raw_even, raw_odd)
 
     def remote(src, dst, send, recv, to_wide, to_rep):
@@ -281,6 +282,18 @@
             partial[j, place, feature] = (mixed[:, :HD] / total).astype(jnp.bfloat16)
             stats_col[place, :] = jnp.where(lane == h, row_max + jnp.log2(total), stats_col[place, :])
 
+    def tables(i, carry):
+        video, own_video = video_ref[i], video_ref[rep]
+        limit = counts_ref[own_video] * (tokens * 8)
+        row, seen = jnp.int32(0), jnp.float32(0.0)
+        for b in range(blocks):
+            held, own = slot_ref[video, b], slot_ref[own_video, b]
+            row += jnp.where(held // rows_held == rep, held % rows_held, 0)
+            seen += jnp.where((own // rows_held == i) & (b * tokens < limit), 1.0, 0.0)
+        sel_ref[i] = row
+        vis_ref[i] = seen
+        return carry
+
     barrier = pltpu.get_barrier_semaphore()
     peers = [(2 * x + h, group_at(k)) for k in range(len(ORDER)) for h in range(2)]
     peers += [(2 * x + other, rep)] + [(2 * to + h, rep) for to in (right, left) for h in range(2)]
@@ -291,6 +304,16 @@
     start(raw_copies(0))
     loads[1].start()
     start(raw_copies(1))
+    loads[0].wait()
+    normalize(0)
+    pl.semaphore_wait(barrier, len(peers))
+    start(first_copies(0))
+    start(first_copies(1))
+    lax.fori_loop(0, groups, tables, 0)
+    gather(0)
+    start(cache_copies(0))
+    gather(1)
+    start(cache_copies(1))
     for h in range(HEADS_CHUNK):
         values[h, 0:quarter, HD:] = jnp.ones((quarter, HD), jnp.bfloat16)
 
@@ -305,15 +328,6 @@
     lax.fori_loop(0, groups, shares, 0)
     stats_col[...] = jnp.zeros_like(stats_col)
     weights_row[...] = jnp.zeros_like(weights_row)
-    gather(0)
-    loads[0].wait()
-    normalize(0)
-    pl.semaphore_wait(barrier, len(peers))
-    start(cache_copies(0))
-    start(first_copies(0))
-    gather(1)
-    start(cache_copies(1))
-    start(first_copies(1))
     loads[1].wait()
     normalize(1)
 
@@ -332,10 +346,6 @@
     start(first_copies(2))
 
     def step(j, carry):
-        @pl.when(j >= 1)
-        def _():
-            forward_partial(j - 1)
-
         wait_hop(j)
         wait_kv(j)
         for copy in own_copies(j):
@@ -373,12 +383,17 @@
 
         @pl.when(j >= 1)
         def _():
-            finish(j - 1)
+            forward_partial(j - 1)
+
+        @pl.when(j >= 2)
+        def _():
+            finish(j - 2)
 
         return carry
 
     lax.fori_loop(0, chunks, step, 0)
     forward_partial(chunks - 1)
+    finish(chunks - 2)
     finish(chunks - 1)
 
     def drain(j, carry):
@@ -399,25 +414,11 @@
 
 
 def body(stretch_qkv, norm_gains, cache, cached_stretches, block_slot, video_of_group):
-    rep = lax.axis_index("rep")
     groups = lax.axis_size("rep")
     _, tokens, _, width = stretch_qkv.shape
     slots = cache.shape[0]
-    blocks = block_slot.shape[1]
     stretch = tokens * lax.axis_size("wide")
-    block_len = cache.shape[2] * lax.axis_size("wide")
-    videos = cached_stretches.shape[0]
     chunks = width // 2 // CHUNK
-    picked = video_of_group[:, None] == jnp.arange(videos, dtype=jnp.int32)[None, :]
-    table = jnp.sum(jnp.where(picked[:, :, None], block_slot[None], 0), axis=1)
-    sel = jnp.sum(jnp.where(table // slots == rep, table % slots, 0), axis=1)
-    mine = jnp.arange(groups, dtype=jnp.int32) == rep
-    own_table = jnp.sum(jnp.where(mine[:, None], table, 0), axis=0)
-    own_count = jnp.sum(jnp.where(mine[:, None] & picked, cached_stretches[None, :], 0))
-    seen = jnp.arange(blocks, dtype=jnp.int32) * block_len < own_count * stretch
-    from_owner = own_table[None, :] // slots == jnp.arange(groups, dtype=jnp.int32)[:, None]
-    vis = jnp.sum(jnp.where(from_owner & seen[None, :], 1.0, 0.0), axis=1)
-
     bf16, f32 = jnp.bfloat16, jnp.float32
     rows_all = stretch
     quarter = 2 * tokens
@@ -430,7 +431,7 @@
         kernel,
         name="attend_exchange",
         out_shape=jax.ShapeDtypeStruct((tokens, width), bf16),
-        in_specs=[smem_spec, smem_spec, any_spec, pl.BlockSpec(memory_space=vmem), any_spec],
+        in_specs=[smem_spec, smem_spec, smem_spec, any_spec, pl.BlockSpec(memory_space=vmem), any_spec],
         out_specs=any_spec,
         scratch_shapes=[
             vmem((2, tokens, width), bf16),
@@ -451,6 +452,8 @@
             vmem((chunks, 2, 8, quarter), f32),
             vmem((chunks, 2, 8, quarter), f32),
             vmem((128, quarter), f32),
+            pltpu.SMEM((groups,), jnp.int32),
+            pltpu.SMEM((groups,), f32),
             dma((2,)),
             dma((2, 2)),
             dma((chunks, 3)),
@@ -471,7 +474,7 @@
             dma((chunks,)),
         ],
         compiler_params=pltpu.CompilerParams(collective_id=0, has_side_effects=True, vmem_limit_bytes=67043328),
-    )(sel, vis, jnp.transpose(stretch_qkv[0], (1, 0, 2)), norm_gains, cache.reshape(slots, 2, 3, 8, width))
+    )(cached_stretches, block_slot, video_of_group, jnp.transpose(stretch_qkv[0], (1, 0, 2)), norm_gains, cache.reshape(slots, 2, 3, 8, width))
     return out[None]
 
 

time: 164 us -> 151 us (0.921)
  Pallas kernels: 157 us -> 148 us
  other arithmetic: 3.68 us -> 0 us
    pallas_call x1, Pallas kernels: 157 us -> 148 us  [body(): pl.pallas_call(kernel, name='attend_exchange', out_shape=jax.ShapeDtypeSt...]
    reduce_sum x3 -> x0, other arithmetic: 2.93 us -> none  [the longest x1 1.47 us: body(): own_table = jnp.sum(jnp.where(mine[:, None], table, 0), axis=0)]
where the time goes in v2:
time: 151 us
  Pallas kernels  148 us (98%)
  local copies, waits for them, and re-layouts  2.94 us (2%)
    pallas_call x1, Pallas kernels, body(): pl.pallas_call(kernel, name='attend_exchange', out_shape=jax.ShapeDtypeSt...  148 us

profile of v2, /device:TPU:1, one launch (start us, length us, event | category | flops | bytes accessed | tf_op | source)
XLA Modules:
  0.0 151.3 jit_solution(16398780313688323441)
XLA Ops:
  0.0 148.3 %attend_exchange.1 = bf16[192,5120]{1,0:T(8,128)(2,1)} custom-call(s32[16]{0:T(128)} %counts_ref.1, s32[16,16]{1,0:T(8,128)} %slot_ref.1, s32[16]{0:T(128)} %video_ref.1, bf16[3,192,5120]{2,1,0:T(8,128)(2,1)} %bitcast.7, f32[2,5120]{1,0:T(2,128)} %gains_ref.1, bf16[16,2,3,8,5120]{4,3,2,1,0:T(8,128)(2,1)} %bitcast.5), custom_call_target="tpu_custom_call" | custom-call | tf_op jit(solution)/shard_map/attend_exchange/pallas_call | solution.py:430
  148.4 2.9 %copy.8 = bf16[1,192,5120]{2,1,0:T(8,128)(2,1)} copy(bf16[1,192,5120]{2,1,0:T(8,128)(2,1)} %bitcast.6) | data formatting | bytes 3932160

commit v3 on v2

--- a/solution.py
+++ b/solution.py
@@ -27,7 +27,7 @@
     qk, raw_even, raw_odd, gathered, arrived, queries, keys_new, values_new, keys, values, partial, relay_in, final_in,
     stats_col, stats, relay_stats, final_stats, weights_row, sel_ref, vis_ref,
     load_sem, raw_sem, own_sem, cache_send, cache_recv, first_send, first_recv, hop_send, hop_recv,
-    kv_send, kv_recv, s1_send, s1_recv, s2_send, s2_recv, out_send, out_recv, out_own,
+    kv_send, kv_recv, s1_send, s1_recv, s2_send, s2_recv, out_send, out_recv, out_own, rows_sem,
 ):
     wide, rep = lax.axis_index("wide"), lax.axis_index("rep")
     x, core = wide // 2, wide % 2
@@ -295,7 +295,8 @@
         return carry
 
     barrier = pltpu.get_barrier_semaphore()
-    peers = [(2 * x + h, group_at(k)) for k in range(len(ORDER)) for h in range(2)]
+    column = [(wide, ((y + d) % 4) * 4 + z) for d in range(1, 4)]
+    peers = [(2 * x + h, y * 4 + (z + d) % 4) for d in range(1, 4) for h in range(2)] + column
     peers += [(2 * x + other, rep)] + [(2 * to + h, rep) for to in (right, left) for h in range(2)]
     for peer in peers:
         pl.semaphore_signal(barrier, inc=1, device_id=peer, device_id_type=MESH)
@@ -304,13 +305,16 @@
     start(raw_copies(0))
     loads[1].start()
     start(raw_copies(1))
+    lax.fori_loop(0, groups, tables, 0)
     loads[0].wait()
     normalize(0)
     pl.semaphore_wait(barrier, len(peers))
+    for peer in column:
+        pl.semaphore_signal(rows_sem, inc=1, device_id=peer, device_id_type=MESH)
     start(first_copies(0))
     start(first_copies(1))
-    lax.fori_loop(0, groups, tables, 0)
     gather(0)
+    pl.semaphore_wait(rows_sem, len(column))
     start(cache_copies(0))
     gather(1)
     start(cache_copies(1))
@@ -411,6 +415,39 @@
         return carry
 
     lax.fori_loop(0, chunks, drain, 0)
+
+
+def deliver_kernel(src_ref, dst_ref, held, in_sem, out_sem):
+    parts = held.shape[0]
+    rows = held.shape[1]
+    loads = [pltpu.make_async_copy(src_ref.at[i * rows : (i + 1) * rows], held.at[i], in_sem.at[i]) for i in range(parts)]
+    stores = [pltpu.make_async_copy(held.at[i], dst_ref.at[i * rows : (i + 1) * rows], out_sem.at[i]) for i in range(parts)]
+    for load in loads:
+        load.start()
+    for load, store in zip(loads, stores):
+        load.wait()
+        store.start()
+    for store in stores:
+        store.wait()
+
+
+def deliver(array):
+    parts = 6
+    rows, width = array.shape
+    any_spec = pl.BlockSpec(memory_space=pl.ANY)
+    return pl.pallas_call(
+        deliver_kernel,
+        name="deliver",
+        out_shape=jax.ShapeDtypeStruct(array.shape, array.dtype),
+        in_specs=[any_spec],
+        out_specs=any_spec,
+        scratch_shapes=[
+            pltpu.VMEM((parts, rows // parts, width), array.dtype),
+            pltpu.SemaphoreType.DMA((parts,)),
+            pltpu.SemaphoreType.DMA((parts,)),
+        ],
+        compiler_params=pltpu.CompilerParams(vmem_limit_bytes=60 << 20),
+    )(array)
 
 
 def body(stretch_qkv, norm_gains, cache, cached_stretches, block_slot, video_of_group):
@@ -472,10 +509,11 @@
             dma((chunks,)),
             dma((chunks,)),
             dma((chunks,)),
+            pltpu.SemaphoreType.REGULAR,
         ],
         compiler_params=pltpu.CompilerParams(collective_id=0, has_side_effects=True, vmem_limit_bytes=67043328),
     )(cached_stretches, block_slot, video_of_group, jnp.transpose(stretch_qkv[0], (1, 0, 2)), norm_gains, cache.reshape(slots, 2, 3, 8, width))
-    return out[None]
+    return deliver(out)[None]
 
 
 def solution(mesh):

time: 151 us -> 149 us (0.987)
  local copies, waits for them, and re-layouts: 2.94 us -> 0 us
    unnamed x1 -> x0, local copies, waits for them, and re-layouts: 2.94 us -> none
    pallas_call x0 -> x1, Pallas kernels: none -> 2.34 us  [deliver(): pl.pallas_call(deliver_kernel, name='deliver', out_shape=jax.ShapeDtypeSt...]
    pallas_call x1, Pallas kernels: 148 us -> 146 us  [body(): pl.pallas_call(kernel, name='attend_exchange', out_shape=jax.ShapeDtypeSt...]
where the time goes in v3:
time: 149 us
  Pallas kernels  149 us (100%)
    pallas_call x1, Pallas kernels, body(): pl.pallas_call(kernel, name='attend_exchange', out_shape=jax.ShapeDtypeSt...  146 us

profile of v3, /device:TPU:1, one launch (start us, length us, event | category | flops | bytes accessed | tf_op | source)
XLA Modules:
  0.0 148.7 jit_solution(4084080885466522702)
XLA Ops:
  0.0 146.4 %attend_exchange.1.src_ref = bf16[192,5120]{1,0:T(8,128)(2,1)} custom-call(s32[16]{0:T(128)} %counts_ref.1, s32[16,16]{1,0:T(8,128)} %slot_ref.1, s32[16]{0:T(128)} %video_ref.1, bf16[3,192,5120]{2,1,0:T(8,128)(2,1)} %bitcast.6, f32[2,5120]{1,0:T(2,128)} %gains_ref.1, bf16[16,2,3,8,5120]{4,3,2,1,0:T(8,128)(2,1)} %bitcast.5), custom_call_target="tpu_custom_call" | custom-call | tf_op jit(solution)/shard_map/attend_exchange/pallas_call | solution.py:467
  146.4 2.3 %deliver.1 = bf16[192,5120]{1,0:T(8,128)(2,1)} custom-call(bf16[192,5120]{1,0:T(8,128)(2,1)} %attend_exchange.1.src_ref), custom_call_target="tpu_custom_call" | custom-call | tf_op jit(solution)/shard_map/deliver/pallas_call | solution.py:438

commit v4 on v3

--- a/solution.py
+++ b/solution.py
@@ -25,7 +25,7 @@
 def kernel(
     counts_ref, slot_ref, video_ref, qkv_ref, gains_ref, cache_ref, out_ref,
     qk, raw_even, raw_odd, gathered, arrived, queries, keys_new, values_new, keys, values, partial, relay_in, final_in,
-    stats_col, stats, relay_stats, final_stats, weights_row, sel_ref, vis_ref,
+    stats_col, stats, relay_stats, final_stats, weights_row, columns_row, sel_ref, vis_ref,
     load_sem, raw_sem, own_sem, cache_send, cache_recv, first_send, first_recv, hop_send, hop_recv,
     kv_send, kv_recv, s1_send, s1_recv, s2_send, s2_recv, out_send, out_recv, out_own, rows_sem,
 ):
@@ -204,8 +204,8 @@
             token = lax.broadcasted_iota(jnp.int32, here.shape, 1)
             merged = token >= tokens if slot == 0 else token < tokens
             stats[j, to] = jnp.where(merged, top + jnp.log2(total), here)
-            weights_row[0:8] = a / total
-            weights_row[8:16] = b / total
+            weights_row[0:HEADS_CHUNK] = a / total
+            weights_row[8 : 8 + HEADS_CHUNK] = b / total
             part = 1 - slot
             columns = jnp.transpose(weights_row[...])[part * tokens : (part + 1) * tokens]
             place = half_rows(to, part)
@@ -232,18 +232,21 @@
         top = jnp.maximum(here, jnp.maximum(first, second))
         a, b, c = jnp.exp2(here - top), jnp.exp2(first - top), jnp.exp2(second - top)
         total = a + b + c
-        weights_row[0:8] = a / total
-        weights_row[8:16] = b / total
-        weights_row[16:24] = c / total
-        columns = jnp.transpose(weights_row[...])
-        place = quarter_rows(x)
-        for h in range(HEADS_CHUNK):
-            feature = slice(h * HD, (h + 1) * HD)
-            mixed = columns[:, h : h + 1] * partial[j, place, feature].astype(jnp.float32)
-            mixed += columns[:, 8 + h : 9 + h] * final_in[j, 0, :, feature].astype(jnp.float32)
-            mixed += columns[:, 16 + h : 17 + h] * final_in[j, 1, :, feature].astype(jnp.float32)
-            partial[j, place, feature] = mixed.astype(jnp.bfloat16)
-        start(out_copies(j))
+        weights_row[0:HEADS_CHUNK] = a / total
+        weights_row[8 : 8 + HEADS_CHUNK] = b / total
+        weights_row[16 : 16 + HEADS_CHUNK] = c / total
+        columns_row[...] = jnp.transpose(weights_row[...])
+        copies = out_copies(j)
+        for copy, part in zip(copies, (other, core)):
+            place, within = half_rows(x, part), token_rows(part)
+            columns = columns_row[within]
+            for h in range(HEADS_CHUNK):
+                feature = slice(h * HD, (h + 1) * HD)
+                mixed = columns[:, h : h + 1] * partial[j, place, feature].astype(jnp.float32)
+                mixed += columns[:, 8 + h : 9 + h] * final_in[j, 0, within, feature].astype(jnp.float32)
+                mixed += columns[:, 16 + h : 17 + h] * final_in[j, 1, within, feature].astype(jnp.float32)
+                partial[j, place, feature] = mixed.astype(jnp.bfloat16)
+            copy.start()
 
     def prepare(j):
         keys[0:quarter] = keys_new[j]
@@ -305,7 +308,6 @@
     start(raw_copies(0))
     loads[1].start()
     start(raw_copies(1))
-    lax.fori_loop(0, groups, tables, 0)
     loads[0].wait()
     normalize(0)
     pl.semaphore_wait(barrier, len(peers))
@@ -313,6 +315,7 @@
         pl.semaphore_signal(rows_sem, inc=1, device_id=peer, device_id_type=MESH)
     start(first_copies(0))
     start(first_copies(1))
+    lax.fori_loop(0, groups, tables, 0)
     gather(0)
     pl.semaphore_wait(rows_sem, len(column))
     start(cache_copies(0))
@@ -382,7 +385,7 @@
 
         lax.fori_loop(1, HEADS_CHUNK, rest, 0)
         for d in range(4):
-            stats[j, d] = jnp.transpose(stats_col[d * quarter : (d + 1) * quarter, :])[0:8]
+            stats[j, d] = jnp.transpose(stats_col[d * quarter : (d + 1) * quarter, :])[0:HEADS_CHUNK]
         start(s1_copies(j))
 
         @pl.when(j >= 1)
@@ -398,23 +401,39 @@
     lax.fori_loop(0, chunks, step, 0)
     forward_partial(chunks - 1)
     finish(chunks - 2)
-    finish(chunks - 1)
-
-    def drain(j, carry):
-        @pl.when(j + SLOTS >= chunks)
-        def _():
-            for copy in cache_copies(j):
-                copy.wait_send()
-
-        for copy in first_copies(j) + hop_copies(j) + kv_copies(j) + s1_copies(j) + s2_copies(j, 0) + s2_copies(j, 1):
-            copy.wait_send()
+
+    def settle(j):
         sent, kept = out_copies(j)
         sent.wait_send()
         sent.wait_recv()
         kept.wait()
+
+    def drain(j, carry):
+        @pl.when(j + SLOTS >= chunks)
+        def _():
+            for copy in cache_copies(j):
+                copy.wait_send()
+
+        for copy in first_copies(j) + hop_copies(j) + kv_copies(j) + s1_copies(j):
+            copy.wait_send()
+
+        @pl.when(j + 1 < chunks)
+        def _():
+            for copy in s2_copies(j, 0) + s2_copies(j, 1):
+                copy.wait_send()
+
+        @pl.when(j + 2 < chunks)
+        def _():
+            settle(j)
+
         return carry
 
     lax.fori_loop(0, chunks, drain, 0)
+    finish(chunks - 1)
+    for copy in s2_copies(chunks - 1, 0) + s2_copies(chunks - 1, 1):
+        copy.wait_send()
+    settle(chunks - 2)
+    settle(chunks - 1)
 
 
 def deliver_kernel(src_ref, dst_ref, held, in_sem, out_sem):
@@ -485,10 +504,11 @@
             vmem((chunks, 2, tokens, CHUNK), bf16),
             vmem((chunks, 2, quarter, CHUNK), bf16),
             vmem((rows_all, 128), f32),
-            vmem((chunks, 4, 8, quarter), f32),
-            vmem((chunks, 2, 8, quarter), f32),
-            vmem((chunks, 2, 8, quarter), f32),
+            vmem((chunks, 4, HEADS_CHUNK, quarter), f32),
+            vmem((chunks, 2, HEADS_CHUNK, quarter), f32),
+            vmem((chunks, 2, HEADS_CHUNK, quarter), f32),
             vmem((128, quarter), f32),
+            vmem((quarter, 128), f32),
             pltpu.SMEM((groups,), jnp.int32),
             pltpu.SMEM((groups,), f32),
             dma((2,)),

time: 149 us -> 149 us (level)
  no operation moved by 1% of the time
where the time goes in v4:
time: 149 us
  Pallas kernels  149 us (100%)
    pallas_call x1, Pallas kernels, body(): pl.pallas_call(kernel, name='attend_exchange', out_shape=jax.ShapeDtypeSt...  147 us

profile of v4, /device:TPU:1, one launch (start us, length us, event | category | flops | bytes accessed | tf_op | source)
XLA Modules:
  0.0 148.9 jit_solution(2266801800540808165)
XLA Ops:
  0.0 146.6 %attend_exchange.1.src_ref = bf16[192,5120]{1,0:T(8,128)(2,1)} custom-call(s32[16]{0:T(128)} %counts_ref.1, s32[16,16]{1,0:T(8,128)} %slot_ref.1, s32[16]{0:T(128)} %video_ref.1, bf16[3,192,5120]{2,1,0:T(8,128)(2,1)} %bitcast.6, f32[2,5120]{1,0:T(2,128)} %gains_ref.1, bf16[16,2,3,8,5120]{4,3,2,1,0:T(8,128)(2,1)} %bitcast.5), custom_call_target="tpu_custom_call" | custom-call | tf_op jit(solution)/shard_map/attend_exchange/pallas_call | solution.py:486
  146.6 2.3 %deliver.1 = bf16[192,5120]{1,0:T(8,128)(2,1)} custom-call(bf16[192,5120]{1,0:T(8,128)(2,1)} %attend_exchange.1.src_ref), custom_call_target="tpu_custom_call" | custom-call | tf_op jit(solution)/shard_map/deliver/pallas_call | solution.py:457
